TPU v7x, 128 devices: a whole 4x4x4 slice. The times are simulated.
128 devices in a mesh: tab: 32 (over x, y, core), rep: 4 (over z).
Axes of the slice: x: 4, y: 4, z: 4, core: 2. Of those that a mesh axis runs over, the one named last changes fastest.
Arguments:
- pooled: bfloat16 [64, 16384, 128], P('tab', 'rep'), may hold values from -6 to 6
- widths: int32 [64], replicated, may hold values from 16 to 128, as said below
- placement: int32 [64], replicated, may hold values from 0 to 63, each once
- route: int32 [4, 4096], P('rep'), may hold values from 0 to 4095, each once within a row
- labels: int32 [4, 4096], P('rep'), may hold values 0 or 1
- proj: bfloat16 [64, 128, 32], replicated, may hold values from -0.5 to 0.5
- senet_in: float32 [64, 32], replicated, may hold values from -6 to 6
- senet_out: float32 [32, 64], replicated, may hold values from -1 to 1
- bilinear: float32 [32, 32], replicated, may hold values from -1 to 1
- w_first: bfloat16 [4096, 256], replicated, may hold values from -0.09375 to 0.09375
- w_second: bfloat16 [256, 256], replicated, may hold values from -0.75 to 0.75
- w_last: bfloat16 [256], replicated, may hold values from -0.375 to 0.375
Outputs:
- scores: float32 [4, 4096], P('rep', 'tab')
- d_pooled: bfloat16 [64, 16384, 128], P('tab', 'rep')
- d_proj: float32 [64, 128, 32], P('tab')
- d_senet_in: float32 [64, 32], replicated
- d_senet_out: float32 [32, 64], replicated
- d_bilinear: float32 [32, 32], replicated
- d_first: float32 [4096, 256], P('tab')
- d_second: float32 [256, 256], replicated
- d_last: float32 [256], replicated
Inputs may be any that keep to these rules, and one draw needn't show every extreme that they name: `widths`: each field's width is 128, 64, 32 or 16. `placement`: a permutation of the fields. `route`: each row is a permutation of 0 to 4095.
All inputs are finite; a program needn't handle non-finite values. No bound on the sum of `labels` on one device may be relied on, other than what follows from the above.
Results may differ from a plain program's by a relative error of at most 0.017.
Values may be sent and summed in bfloat16 or wider, within the bound.
A program may use at most 64 MiB of HBM per device.

v0:
```python
import jax
import jax.numpy as jnp
from jax import lax
from jax.sharding import PartitionSpec as P


def sent_to_all(value, axis):
    peers = lax.axis_size(axis)
    return lax.all_to_all(
        jnp.broadcast_to(value[None], (peers, *value.shape)), axis, 0, 0, tiled=True
    )


def of_everyone(value, axis):
    everything = sent_to_all(value, axis)
    return jnp.sum(everything.astype(jnp.float32), axis=0)


def laid_out(pieces, dim):
    lengths = list(pieces.shape[1:])
    lengths[dim] *= pieces.shape[0]
    return jnp.moveaxis(pieces, 0, dim).reshape(lengths)


def collect(value, axis, dim):
    pieces = sent_to_all(value, axis)
    return laid_out(pieces, dim)


def silu_slope(pre_act):
    logistic = jax.nn.sigmoid(pre_act)
    return logistic * (1.0 + pre_act * (1.0 - logistic))


def bilinear_forward(fields_in, bilinear, factor):
    product = jnp.einsum("fnc,cd->fnd", fields_in, bilinear)
    others = jnp.sum(fields_in, axis=0, keepdims=True) - fields_in
    return (product * others * factor, product, others)


def bilinear_backward(fields_in, product, others, upstream, bilinear, factor):
    d_product = upstream * others * factor
    d_others = upstream * product * factor
    d_fields = jnp.einsum("fnd,cd->fnc", d_product, bilinear)
    d_fields = d_fields + jnp.sum(d_others, axis=0, keepdims=True) - d_others
    d_weight = jnp.einsum("fnc,fnd->cd", fields_in, d_product)
    return (d_fields, d_weight)


def owner_pass(embeds, targets, senet_in, senet_out, bilinear, w_first, w_second, w_last):
    count = embeds.shape[0]
    width = embeds.shape[2]
    hidden = w_second.shape[0]
    factor = count ** (-0.5)
    first = w_first.reshape(2, count, width, hidden)
    dense = embeds.astype(jnp.float32)
    squeeze = jnp.mean(dense, axis=2)
    pre_one = jnp.einsum("fn,fr->rn", squeeze, senet_in)
    act_one = jax.nn.silu(pre_one)
    pre_two = jnp.einsum("rn,rf->fn", act_one, senet_out)
    weights = jax.nn.sigmoid(pre_two)
    scaled = weights[:, :, None] * dense
    plain_out, plain_prod, plain_rest = bilinear_forward(dense, bilinear, factor)
    scaled_out, scaled_prod, scaled_rest = bilinear_forward(scaled, bilinear, factor)
    joined = jnp.stack([plain_out, scaled_out]).astype(jnp.bfloat16)
    pre_hidden = jnp.einsum("kfnc,kfch->nh", joined, first, preferred_element_type=jnp.float32)
    hidden_one = jax.nn.silu(pre_hidden).astype(jnp.bfloat16)
    pre_second = jnp.dot(hidden_one, w_second, preferred_element_type=jnp.float32)
    hidden_two = jax.nn.silu(pre_second).astype(jnp.bfloat16)
    logits = jnp.dot(hidden_two, w_last, preferred_element_type=jnp.float32)
    grad_logit = jax.nn.sigmoid(logits) - targets
    d_last = jnp.dot(grad_logit, hidden_two.astype(jnp.float32))
    last_wide = w_last.astype(jnp.float32)
    d_pre_two = (grad_logit[:, None] * last_wide[None, :] * silu_slope(pre_second)).astype(
        jnp.bfloat16
    )
    d_second = jnp.dot(hidden_one.T, d_pre_two, preferred_element_type=jnp.float32)
    back_two = jnp.dot(d_pre_two, w_second.T, preferred_element_type=jnp.float32)
    d_pre_one = (back_two * silu_slope(pre_hidden)).astype(jnp.bfloat16)
    d_first = jnp.einsum(
        "kfnc,nh->kfch", joined, d_pre_one, preferred_element_type=jnp.float32
    ).reshape(-1, hidden)
    d_joined = jnp.einsum("nh,kfch->kfnc", d_pre_one, first, preferred_element_type=jnp.float32)
    d_plain, d_bil_plain = bilinear_backward(
        dense, plain_prod, plain_rest, d_joined[0], bilinear, factor
    )
    d_scaled, d_bil_scaled = bilinear_backward(
        scaled, scaled_prod, scaled_rest, d_joined[1], bilinear, factor
    )
    d_weights = jnp.sum(d_scaled * dense, axis=2)
    d_pre_w = d_weights * weights * (1.0 - weights)
    d_senet_out = jnp.einsum("rn,fn->rf", act_one, d_pre_w)
    d_act = jnp.einsum("fn,rf->rn", d_pre_w, senet_out) * silu_slope(pre_one)
    d_senet_in = jnp.einsum("fn,rn->fr", squeeze, d_act)
    d_squeeze = jnp.einsum("rn,fr->fn", d_act, senet_in)
    d_embeds = d_plain + weights[:, :, None] * d_scaled + d_squeeze[:, :, None] / width
    small = (d_senet_in, d_senet_out, d_bil_plain + d_bil_scaled, d_second, d_last)
    return (logits, d_embeds.astype(jnp.bfloat16), small, d_first, joined, d_pre_one)


def shards(
    pooled,
    widths,
    placement,
    route,
    labels,
    proj,
    senet_in,
    senet_out,
    bilinear,
    w_first,
    w_second,
    w_last,
):
    tab_count = lax.axis_size("tab")
    tab_index = lax.axis_index("tab")
    local_count = pooled.shape[0]
    rep_rows = pooled.shape[1]
    padded = pooled.shape[2]
    field_count = placement.shape[0]
    owner_rows = rep_rows // tab_count
    field_ids = jnp.arange(field_count, dtype=jnp.int32)
    matches = placement[:, None] == field_ids[None, :]
    slot_width = jnp.sum(jnp.where(matches, widths[None, :], 0), axis=1)
    slot_mask = (jnp.arange(padded, dtype=jnp.int32)[None, :] < slot_width[:, None]).astype(
        jnp.bfloat16
    )
    inverse = jnp.zeros_like(placement).at[placement].set(field_ids)
    targets = lax.dynamic_slice_in_dim(labels[0], tab_index * owner_rows, owner_rows).astype(
        jnp.float32
    )
    first_slot = tab_index * local_count
    local_fields = lax.dynamic_slice_in_dim(placement, first_slot, local_count)
    local_mask = lax.dynamic_slice_in_dim(slot_mask, first_slot, local_count, 0)
    local_proj = jnp.take(proj, local_fields, axis=0)
    masked = pooled * local_mask[:, None, :]
    embed_local = jnp.einsum(
        "fnc,fcd->fnd", masked, local_proj, preferred_element_type=jnp.float32
    ).astype(jnp.bfloat16)
    embed_slot = lax.all_to_all(embed_local, "tab", split_axis=1, concat_axis=0, tiled=True)
    logits, d_embeds, small, d_first_part, joined, d_pre_one = owner_pass(
        embed_slot[inverse], targets, senet_in, senet_out, bilinear, w_first, w_second, w_last
    )
    d_slot = d_embeds[placement]
    d_local = lax.all_to_all(d_slot, "tab", split_axis=0, concat_axis=1, tiled=True)
    back = jnp.einsum("fnd,fcd->fnc", d_local, local_proj, preferred_element_type=jnp.float32)
    back = (back * local_mask[:, None, :]).astype(jnp.bfloat16)
    d_proj_part = jnp.einsum("fnc,fnd->fcd", masked, d_local, preferred_element_type=jnp.float32)
    d_proj = of_everyone(d_proj_part.astype(jnp.bfloat16), "rep").astype(jnp.float32)
    first_tab = lax.psum_scatter(
        d_first_part.astype(jnp.bfloat16), "tab", scatter_dimension=0, tiled=True
    )
    d_first = of_everyone(first_tab, "rep").astype(jnp.float32)
    part_in, part_out, part_bil, part_second, part_last = small
    d_senet_in, d_senet_out, d_bilinear, d_second, d_last = lax.psum(
        (part_in, part_out, part_bil, part_second, part_last), ("tab", "rep")
    )
    all_logits = collect(logits, "tab", 0)
    wanted = lax.dynamic_slice_in_dim(route[0], tab_index * owner_rows, owner_rows)
    scores = jnp.take(all_logits, wanted)[None, :]
    return (scores, back, d_proj, d_senet_in, d_senet_out, d_bilinear, d_first, d_second, d_last)


def solution(mesh):
    placed = (
        P("tab", "rep", None),
        P(),
        P(),
        P("rep", None),
        P("rep", None),
        P(),
        P(),
        P(),
        P(),
        P(),
        P(),
        P(),
    )
    return jax.shard_map(
        shards,
        mesh=mesh,
        in_specs=placed,
        out_specs=(
            P("rep", "tab"),
            P("tab", "rep", None),
            P("tab", None, None),
            P(),
            P(),
            P(),
            P("tab", None),
            P(),
            P(),
        ),
        check_vma=False,
    )
```

profile of v0, /device:TPU:1, one launch (start us, length us, event | category | flops | bytes accessed | tf_op | source)
XLA Modules:
  0.0 225.5 jit_solution(7572727441180644628)
XLA Ops:
  8.0 1.0 select_reduce_fusion
  9.9 1.6 gather_fusion
  11.5 2.4 %convolution_convert_fusion = bf16[2,4096,32]{1,2,0:T(8,128)(2,1)S(1)} fusion(bf16[2,4096,128]{2,1,0:T(8,128)(2,1)} %param.12, bf16[2,128]{1,0:T(2,128)(2,1)S(1)} %get-tuple-element.22, bf16[2,128,32]{1,2,0:T(8,128)(2,1)S(1)} %gather_fusion, pred[2]{0:T(512)(128)(4,1)S(1)} %get-tuple-element.17), kind=kOutput, calls=%fused_computation.7 | convolution fusion | flops 68427776 | bytes 2638338 | tf_op jit(solution)/shard_map/fnc,fcd->fnd/dot_general | solution.py:137
  14.0 3.8 %copy.56 = bf16[2,4096,32]{2,0,1:T(2,128)(2,1)} copy(bf16[2,4096,32]{1,2,0:T(8,128)(2,1)S(1)} %convolution_convert_fusion) | data formatting | bytes 1048576 | tf_op jit(solution)/shard_map/convert_element_type | solution.py:139
  17.8 5.9 %reshape.152 = bf16[32,2,4096]{2,1,0:T(2,128)(2,1)} reshape(bf16[4096,2,32]{2,1,0:T(2,128)(2,1)} %bitcast.166) | data formatting | bytes 1048576
  23.7 8.6 %all-to-all-start = ((bf16[32,2,4096]{2,1,0:T(2,128)(2,1)}), bf16[32,2,4096]{2,1,0:T(2,128)(2,1)S(1)}, u32[]{:S(2)}, u32[]{:S(2)}) async-start(bf16[32,2,4096]{2,1,0:T(2,128)(2,1)} %reshape.152), calls=%async_computation | async-start | bytes 1048576 | tf_op jit(solution)/shard_map/all_to_all | solution.py:140
  32.4 0.8 scatter_custom_fusion
  33.2 10.7 %all-to-all-done = bf16[32,2,4096]{2,1,0:T(2,128)(2,1)S(1)} async-done(((bf16[32,2,4096]{2,1,0:T(2,128)(2,1)}), bf16[32,2,4096]{2,1,0:T(2,128)(2,1)S(1)}, u32[]{:S(2)}, u32[]{:S(2)}) %all-to-all-start) | async-done | bytes 524320 | tf_op jit(solution)/shard_map/all_to_all | solution.py:140
  43.9 2.0 reshape.153
  45.8 4.7 %copy.73 = bf16[2,32,128,32]{2,3,0,1:T(8,128)(2,1)S(1)} copy(bf16[2,32,128,32]{3,0,2,1:T(2,128)(2,1)} %bitcast.167) | data formatting | bytes 1048576 | tf_op jit(solution)/shard_map/all_to_all | solution.py:140
  54.3 0.8 divide_subtract_fusion
  55.4 2.0 convolution_convert_fusion.1
  58.7 3.6 %all-to-all-start.1 = ((f32[32,1,128]{2,1,0:T(1,128)}), f32[32,1,128]{2,1,0:T(1,128)S(1)}, u32[]{:S(2)}, u32[]{:S(2)}) async-start(f32[32,1,128]{2,1,0:T(1,128)} %broadcast_in_dim.45), calls=%async_computation.1 | async-start | bytes 32768 | tf_op jit(solution)/shard_map/all_to_all | solution.py:9
  63.5 1.7 copy-done.3
  66.0 1.5 fusion.41
  68.1 1.0 fusion.99
  69.1 2.7 %fusion.14 = bf16[64,128,32]{1,2,0:T(8,128)(2,1)S(1)} fusion(f32[64,128,32]{1,2,0:T(8,128)} %get-tuple-element.28, bf16[64,128,32]{1,2,0:T(8,128)(2,1)S(1)} %gather_fusion.1, f32[2,64,128,32]{2,3,1,0:T(8,128)} %copy-done.1, f32[64,128]{1,0:T(8,128)S(1)} %fusion.24, f32[128,32]{0,1:T(8,128)S(1)} %get-tuple-element.9, f32[64,128]{1,0:T(8,128)S(1)} %fusion.28, ...), kind=kOutput, calls=%fused_computation.30 | convolution fusion | flops 19922944 | bytes 5345280 | tf_op jit(solution)/shard_map/fnd,cd->fnc/dot_general | solution.py:44
  71.8 1.4 gather_fusion.3
  73.2 7.4 %all-to-all-start.2 = ((bf16[64,128,32]{1,2,0:T(8,128)(2,1)}), bf16[64,128,32]{1,2,0:T(8,128)(2,1)S(1)}, u32[]{:S(2)}, u32[]{:S(2)}) async-start(bf16[64,128,32]{1,2,0:T(8,128)(2,1)} %gather_fusion.3), calls=%async_computation.2 | async-start | bytes 1048576 | tf_op jit(solution)/shard_map/all_to_all | solution.py:145
  80.7 1.6 fusion.34
  82.4 68.8 %all-reduce = (f32[64,32]{0,1:T(8,128)}, f32[32,64]{1,0:T(8,128)}, f32[32,32]{1,0:T(8,128)}, f32[256]{0:T(256)}) all-reduce(f32[64,32]{0,1:T(8,128)S(1)} %fusion.68, f32[32,64]{1,0:T(8,128)S(1)} %fusion.79, f32[32,32]{1,0:T(8,128)S(1)} %fusion.34, f32[256]{0:T(256)S(1)} %bitcast.171), channel_id=1, replica_groups=mesh['tab'=32,'rep'=4] {'tab','rep'}, use_global_device_ids=true, to_apply=%region_9.10 | all-reduce | flops 5376 | bytes 43008 | tf_op jit(solution)/shard_map/psum | solution.py:155
  151.2 1.1 gather_fusion.2
  152.4 2.2 fusion.29
  155.2 3.3 %all-to-all-start.3 = ((bf16[4,2,128,32]{2,3,1,0:T(8,128)(2,1)}), bf16[4,2,128,32]{2,3,1,0:T(8,128)(2,1)S(1)}, u32[]{:S(2)}, u32[]{:S(2)}) async-start(bf16[4,2,128,32]{2,3,1,0:T(8,128)(2,1)} %broadcast_in_dim.49), calls=%async_computation.3 | async-start | bytes 131072 | tf_op jit(solution)/shard_map/all_to_all | solution.py:9
  158.5 1.2 and_select_fusion
  159.7 3.3 %all-to-all-done.3 = bf16[4,2,128,32]{2,3,1,0:T(8,128)(2,1)S(1)} async-done(((bf16[4,2,128,32]{2,3,1,0:T(8,128)(2,1)}), bf16[4,2,128,32]{2,3,1,0:T(8,128)(2,1)S(1)}, u32[]{:S(2)}, u32[]{:S(2)}) %all-to-all-start.3) | async-done | bytes 65568 | tf_op jit(solution)/shard_map/all_to_all | solution.py:9
  162.9 1.6 broadcast_in_dim.82
  164.5 3.4 %all-to-all-start.4 = ((bf16[4,128,256]{2,1,0:T(8,128)(2,1)}), bf16[4,128,256]{2,1,0:T(8,128)(2,1)S(1)}, u32[]{:S(2)}, u32[]{:S(2)}) async-start(bf16[4,128,256]{2,1,0:T(8,128)(2,1)} %broadcast_in_dim.82), calls=%async_computation.5 | async-start | bytes 524288 | tf_op jit(solution)/shard_map/all_to_all | solution.py:9
  167.9 2.3 %fusion = bf16[2,4096,128]{2,1,0:T(8,128)(2,1)} fusion(f32[2,128]{1,0:T(2,128)S(1)} %get-tuple-element.21, bf16[32,2,4,8,128]{4,3,2,1,0:T(8,128)(2,1)S(1)} %bitcast.170, bf16[2,128,32]{1,2,0:T(8,128)(2,1)S(1)} %gather_fusion, pred[2]{0:T(512)(128)(4,1)S(1)} %get-tuple-element.17), kind=kOutput, calls=%fused_computation.6 | convolution fusion | flops 69214208 | bytes 2638850 | tf_op jit(solution)/shard_map/fnd,fcd->fnc/dot_general | solution.py:146
  170.8 2.6 %all-to-all-done.4 = bf16[4,128,256]{2,1,0:T(8,128)(2,1)S(1)} async-done(((bf16[4,128,256]{2,1,0:T(8,128)(2,1)}), bf16[4,128,256]{2,1,0:T(8,128)(2,1)S(1)}, u32[]{:S(2)}, u32[]{:S(2)}) %all-to-all-start.4) | async-done | bytes 262176 | tf_op jit(solution)/shard_map/all_to_all | solution.py:9
  174.1 42.3 %all-reduce.3.cloned.1.call-done = f32[256,256]{1,0:T(8,128)} async-done(((f32[256,256]{1,0:T(8,128)}), f32[256,256]{1,0:T(8,128)}) %all-reduce.3.cloned.1.call-update) | async-done | bytes 262160 | tf_op jit(solution)/shard_map/psum | solution.py:155
  216.3 1.7 copy.92
  (66 shorter events, 10.8 us)
Async XLA Ops:
  8.0 45.2 %copy-start = (bf16[4096,256]{1,0:T(8,128)(2,1)S(1)}, bf16[4096,256]{1,0:T(8,128)(2,1)}, u32[]{:S(2)}) copy-start(bf16[4096,256]{1,0:T(8,128)(2,1)} %param.21) | copy-start | bytes 6291460
  17.8 14.5 %copy-start.11 = (bf16[256]{0:T(256)(128)(2,1)S(1)}, bf16[256]{0:T(256)(128)(2,1)}, u32[]{:S(2)}) copy-start(bf16[256]{0:T(256)(128)(2,1)} %param.23) | copy-start | bytes 1540
  17.8 14.5 %copy-start.8 = (s32[64]{0:T(128)S(1)}, s32[64]{0:T(128)}, u32[]{:S(2)}) copy-start(s32[64]{0:T(128)} %param.14) | copy-start | bytes 772
  23.7 20.2 %all-to-all-start = ((bf16[32,2,4096]{2,1,0:T(2,128)(2,1)}), bf16[32,2,4096]{2,1,0:T(2,128)(2,1)S(1)}, u32[]{:S(2)}, u32[]{:S(2)}) async-start(bf16[32,2,4096]{2,1,0:T(2,128)(2,1)} %reshape.152), calls=%async_computation | async-start | bytes 1048576 | tf_op jit(solution)/shard_map/all_to_all | solution.py:140
  32.3 130.7 %reduce-scatter.2.cloned.1.call-start = ((), (), s32[]{:S(2)}) async-start(), calls=%async_computation.6 | async-start | bytes 2162688 | tf_op jit(solution)/shard_map/reduce_scatter | solution.py:150
  50.5 0.8 copy-start.7
  50.5 1.0 copy-start.10
  50.5 1.3 copy-start.6
  52.2 1.0 copy-start.4
  52.6 1.2 copy-start.2
  53.2 0.9 copy-start.9
  58.7 14.5 %all-to-all-start.1 = ((f32[32,1,128]{2,1,0:T(1,128)}), f32[32,1,128]{2,1,0:T(1,128)S(1)}, u32[]{:S(2)}, u32[]{:S(2)}) async-start(f32[32,1,128]{2,1,0:T(1,128)} %broadcast_in_dim.45), calls=%async_computation.1 | async-start | bytes 32768 | tf_op jit(solution)/shard_map/all_to_all | solution.py:9
  62.4 154.0 %all-reduce.3.cloned.1.call-start = ((), (), s32[]{:S(2)}) async-start(), calls=%async_computation.7 | async-start | bytes 524288 | tf_op jit(solution)/shard_map/psum | solution.py:155
  63.1 2.8 %copy-start.1 = (f32[2,64,128,32]{2,3,1,0:T(8,128)}, f32[2,64,128,32]{2,3,1,0:T(8,128)S(1)}, u32[]{:S(2)}) copy-start(f32[2,64,128,32]{2,3,1,0:T(8,128)S(1)} %convolution_bitcast_fusion) | copy-start | bytes 6291460
  63.1 2.0 copy-start.3
  63.1 2.3 %copy-start.5 = (f32[64,128,32]{1,2,0:T(8,128)S(1)}, f32[64,128,32]{1,2,0:T(8,128)}, u32[]{:S(2)}) copy-start(f32[64,128,32]{1,2,0:T(8,128)} %copy-done.4) | copy-start | bytes 3145732
  73.2 79.1 %all-to-all-start.2 = ((bf16[64,128,32]{1,2,0:T(8,128)(2,1)}), bf16[64,128,32]{1,2,0:T(8,128)(2,1)S(1)}, u32[]{:S(2)}, u32[]{:S(2)}) async-start(bf16[64,128,32]{1,2,0:T(8,128)(2,1)} %gather_fusion.3), calls=%async_computation.2 | async-start | bytes 1048576 | tf_op jit(solution)/shard_map/all_to_all | solution.py:145
  155.2 7.7 %all-to-all-start.3 = ((bf16[4,2,128,32]{2,3,1,0:T(8,128)(2,1)}), bf16[4,2,128,32]{2,3,1,0:T(8,128)(2,1)S(1)}, u32[]{:S(2)}, u32[]{:S(2)}) async-start(bf16[4,2,128,32]{2,3,1,0:T(8,128)(2,1)} %broadcast_in_dim.49), calls=%async_computation.3 | async-start | bytes 131072 | tf_op jit(solution)/shard_map/all_to_all | solution.py:9
  164.5 8.9 %all-to-all-start.4 = ((bf16[4,128,256]{2,1,0:T(8,128)(2,1)}), bf16[4,128,256]{2,1,0:T(8,128)(2,1)S(1)}, u32[]{:S(2)}, u32[]{:S(2)}) async-start(bf16[4,128,256]{2,1,0:T(8,128)(2,1)} %broadcast_in_dim.82), calls=%async_computation.5 | async-start | bytes 524288 | tf_op jit(solution)/shard_map/all_to_all | solution.py:9
Sparse Core Ops, SparseCore 0:
  57.6 75.3 reduce-scatter.1
Sparse Core Ops, SparseCore 1:
  69.2 147.1 all-reduce.2
where the time goes:
time: 226 us; the launch traced here: 225 us
  blocking collectives  68.8 us (30%)
  waiting for transfers between devices  58.9 us (26%)
  local copies, waits for them, and re-layouts  29.1 us (13%)
  starting transfers between devices  26.4 us (12%)
  matrix products  20.3 us (9%)
  between operations  15.8 us (7%)
  other arithmetic  6.22 us (3%)
    psum x1, blocking collectives, shards(): lax.psum((part_in, part_out, part_bil, part_second, part_last), ('tab', '...  68.8 us
    psum x1, waiting for transfers between devices, shards(): lax.psum((part_in, part_out, part_bil, part_second, part_last), ('tab', '...  42.3 us
    unnamed x28, local copies, waits for them, and re-layouts  12.1 us
    all_to_all x1, waiting for transfers between devices, shards(): lax.all_to_all(embed_local, 'tab', split_axis=1, concat_axis=0, tiled=True)  10.7 us
    all_to_all x3, starting transfers between devices, sent_to_all(): lax.all_to_all(jnp.broadcast_to(value[None], (peers, *value.shape)), axis...  10.3 us
    all_to_all x1, starting transfers between devices, shards(): lax.all_to_all(embed_local, 'tab', split_axis=1, concat_axis=0, tiled=True)  8.58 us
    all_to_all x1, starting transfers between devices, shards(): lax.all_to_all(d_slot, 'tab', split_axis=0, concat_axis=1, tiled=True)  7.39 us
    all_to_all x3, waiting for transfers between devices, sent_to_all(): lax.all_to_all(jnp.broadcast_to(value[None], (peers, *value.shape)), axis...  5.88 us
  transfers between devices with their start and end apart: 7, of which 4 were waited for; matrix products, arithmetic and copies ran while one was open for 10% of the time, Pallas kernels for 0%

commit v1 on v0

--- a/solution.py
+++ b/solution.py
@@ -153,7 +153,7 @@
     d_first = of_everyone(first_tab, "rep").astype(jnp.float32)
     part_in, part_out, part_bil, part_second, part_last = small
     d_senet_in, d_senet_out, d_bilinear, d_second, d_last = lax.psum(
-        (part_in, part_out, part_bil, part_second, part_last), ("tab", "rep")
+        lax.psum((part_in, part_out, part_bil, part_second, part_last), "tab"), "rep"
     )
     all_logits = collect(logits, "tab", 0)
     wanted = lax.dynamic_slice_in_dim(route[0], tab_index * owner_rows, owner_rows)

time: 226 us -> 292 us (1.29)
  blocking collectives: 68.8 us -> 140 us
  waiting for transfers between devices: 58.9 us -> 53.7 us
    psum x1 -> x2, blocking collectives: 68.8 us -> 140 us  [the longest x1 123 us: shards(): lax.psum((part_in, part_out, part_bil, part_second, part_last), 'tab')]
    psum x1 -> x2, waiting for transfers between devices: 42.3 us -> 31.5 us  [the longest x1 31.5 us: shards(): lax.psum(lax.psum((part_in, part_out, part_bil, part_second, part_last),...]
    reduce_scatter x1, waiting for transfers between devices: 0.01 us -> 5.67 us  [shards(): lax.psum_scatter(d_first_part.astype(jnp.bfloat16), 'tab', scatter_dimens...]
    dot_general x2, matrix products: 4.24 us -> 1.09 us  [bilinear_backward(): d_fields = jnp.einsum('fnd,cd->fnc', d_product, bilinear)]
    unnamed x28 -> x32, local copies, waits for them, and re-layouts: 12.1 us -> 10.7 us
  transfers between devices with their start and end apart: 7 -> 8, of which waited for: 4 -> 6; matrix products, arithmetic and copies ran while one was open for 10% -> 9% of each run, Pallas kernels for 0% -> 0%
where the time goes in v1:
time: 292 us; the launch traced here: 290 us
  blocking collectives  140 us (48%)
  waiting for transfers between devices  53.7 us (18%)
  local copies, waits for them, and re-layouts  27.7 us (9%)
  starting transfers between devices  26.5 us (9%)
  matrix products  19.5 us (7%)
  between operations  14.1 us (5%)
  other arithmetic  8.5 us (3%)
    psum x1, blocking collectives, shards(): lax.psum((part_in, part_out, part_bil, part_second, part_last), 'tab')  123 us
    psum x1, waiting for transfers between devices, shards(): lax.psum(lax.psum((part_in, part_out, part_bil, part_second, part_last),...  31.5 us
    psum x1, blocking collectives, shards(): lax.psum(lax.psum((part_in, part_out, part_bil, part_second, part_last),...  16.2 us
    all_to_all x3, starting transfers between devices, sent_to_all(): lax.all_to_all(jnp.broadcast_to(value[None], (peers, *value.shape)), axis...  11 us
    unnamed x32, local copies, waits for them, and re-layouts  10.7 us
    all_to_all x1, waiting for transfers between devices, shards(): lax.all_to_all(embed_local, 'tab', split_axis=1, concat_axis=0, tiled=True)  9.99 us
    all_to_all x1, starting transfers between devices, shards(): lax.all_to_all(embed_local, 'tab', split_axis=1, concat_axis=0, tiled=True)  8.58 us
    all_to_all x1, starting transfers between devices, shards(): lax.all_to_all(d_slot, 'tab', split_axis=0, concat_axis=1, tiled=True)  6.76 us
  transfers between devices with their start and end apart: 8, of which 6 were waited for; matrix products, arithmetic and copies ran while one was open for 9% of the time, Pallas kernels for 0%

profile of v1, /device:TPU:1, one launch (start us, length us, event | category | flops | bytes accessed | tf_op | source)
XLA Modules:
  0.0 289.8 jit_solution(15388546789475622234)
XLA Ops:
  7.2 1.0 select_reduce_fusion
  9.1 1.6 gather_fusion
  10.7 2.4 convolution_convert_fusion
  13.1 3.8 %copy.56 = bf16[2,4096,32]{2,0,1:T(2,128)(2,1)} copy(bf16[2,4096,32]{1,2,0:T(8,128)(2,1)S(1)} %convolution_convert_fusion) | data formatting | bytes 1048576 | tf_op jit(solution)/shard_map/convert_element_type | solution.py:139
  17.0 5.9 %reshape.152 = bf16[32,2,4096]{2,1,0:T(2,128)(2,1)} reshape(bf16[4096,2,32]{2,1,0:T(2,128)(2,1)} %bitcast.166) | data formatting | bytes 1048576
  22.8 8.6 %all-to-all-start = ((bf16[32,2,4096]{2,1,0:T(2,128)(2,1)}), bf16[32,2,4096]{2,1,0:T(2,128)(2,1)S(1)}, u32[]{:S(2)}, u32[]{:S(2)}) async-start(bf16[32,2,4096]{2,1,0:T(2,128)(2,1)} %reshape.152), calls=%async_computation | async-start | bytes 1048576 | tf_op jit(solution)/shard_map/all_to_all | solution.py:140
  33.0 10.0 %all-to-all-done = bf16[32,2,4096]{2,1,0:T(2,128)(2,1)S(1)} async-done(((bf16[32,2,4096]{2,1,0:T(2,128)(2,1)}), bf16[32,2,4096]{2,1,0:T(2,128)(2,1)S(1)}, u32[]{:S(2)}, u32[]{:S(2)}) %all-to-all-start) | async-done | bytes 524320 | tf_op jit(solution)/shard_map/all_to_all | solution.py:140
  43.0 2.0 reshape.153
  45.0 4.7 %copy.73 = bf16[2,32,128,32]{2,3,0,1:T(8,128)(2,1)S(1)} copy(bf16[2,32,128,32]{3,0,2,1:T(2,128)(2,1)} %bitcast.167) | data formatting | bytes 1048576 | tf_op jit(solution)/shard_map/all_to_all | solution.py:140
  53.6 0.8 divide_subtract_fusion
  54.7 1.0 fusion.99
  55.7 3.1 %convolution_convert_fusion.1 = bf16[2,64,32,256]{3,2,1,0:T(8,128)(2,1)} fusion(bf16[128,256,1,1]{1,0,3,2:T(8,128)(2,1)S(1)} %fusion.23, bf16[1,64,128,32]{2,3,1,0:T(8,128)(2,1)} %copy-done.7, bf16[1,64,128,32]{2,3,1,0:T(8,128)(2,1)S(1)} %get-tuple-element.23), kind=kOutput, calls=%fused_computation.15 | convolution fusion | flops 270008320 | bytes 3211264 | tf_op jit(solution)/shard_map/kfnc,nh->kfch/dot_general | solution.py:80
  58.8 2.0 convolution_bitcast_fusion
  61.4 3.6 %all-to-all-start.1 = ((f32[32,1,128]{2,1,0:T(1,128)}), f32[32,1,128]{2,1,0:T(1,128)S(1)}, u32[]{:S(2)}, u32[]{:S(2)}) async-start(f32[32,1,128]{2,1,0:T(1,128)} %broadcast_in_dim.45), calls=%async_computation.1 | async-start | bytes 32768 | tf_op jit(solution)/shard_map/all_to_all | solution.py:9
  65.1 2.8 fusion.66
  69.9 1.4 gather_fusion.3
  72.0 6.8 %all-to-all-start.2 = ((bf16[64,128,32]{1,2,0:T(8,128)(2,1)}), bf16[64,128,32]{1,2,0:T(8,128)(2,1)S(1)}, u32[]{:S(2)}, u32[]{:S(2)}) async-start(bf16[64,128,32]{1,2,0:T(8,128)(2,1)} %gather_fusion.3), calls=%async_computation.2 | async-start | bytes 1048576 | tf_op jit(solution)/shard_map/all_to_all | solution.py:145
  78.9 1.7 convolution_bitcast_fusion.1
  81.1 123.5 %all-reduce = (f32[64,32]{0,1:T(8,128)S(1)}, f32[32,64]{1,0:T(8,128)S(1)}, f32[32,32]{1,0:T(8,128)S(1)}, f32[256]{0:T(256)S(1)}) all-reduce(f32[64,32]{0,1:T(8,128)S(1)} %fusion.68, f32[32,64]{1,0:T(8,128)S(1)} %fusion.79, f32[32,32]{1,0:T(8,128)S(1)} %fusion.34, f32[256]{0:T(256)S(1)} %bitcast.171), channel_id=1, replica_groups=mesh['tab'=32,'rep'=4] {'tab'}, use_global_device_ids=true, to_apply=%region_9.10 | all-reduce | flops 5376 | bytes 43008 | tf_op jit(solution)/shard_map/psum | solution.py:156
  204.5 16.2 %all-reduce.1 = (f32[64,32]{0,1:T(8,128)}, f32[32,64]{1,0:T(8,128)}, f32[32,32]{1,0:T(8,128)}, f32[256]{0:T(256)}) all-reduce(f32[64,32]{0,1:T(8,128)S(1)} %get-tuple-element.13, f32[32,64]{1,0:T(8,128)S(1)} %get-tuple-element.14, f32[32,32]{1,0:T(8,128)S(1)} %get-tuple-element.15, ...), channel_id=1, replica_groups=mesh['tab'=32,'rep'=4] {'rep'}, use_global_device_ids=true, to_apply=%region_10.11 | all-reduce | flops 5376 | bytes 43008 | tf_op jit(solution)/shard_map/psum | solution.py:155
  220.7 1.1 gather_fusion.2
  221.9 2.2 fusion.29
  224.7 3.3 %all-to-all-start.3 = ((bf16[4,2,128,32]{2,3,1,0:T(8,128)(2,1)}), bf16[4,2,128,32]{2,3,1,0:T(8,128)(2,1)S(1)}, u32[]{:S(2)}, u32[]{:S(2)}) async-start(bf16[4,2,128,32]{2,3,1,0:T(8,128)(2,1)} %broadcast_in_dim.49), calls=%async_computation.3 | async-start | bytes 131072 | tf_op jit(solution)/shard_map/all_to_all | solution.py:9
  228.1 1.2 and_select_fusion
  229.3 3.2 %all-to-all-done.3 = bf16[4,2,128,32]{2,3,1,0:T(8,128)(2,1)S(1)} async-done(((bf16[4,2,128,32]{2,3,1,0:T(8,128)(2,1)}), bf16[4,2,128,32]{2,3,1,0:T(8,128)(2,1)S(1)}, u32[]{:S(2)}, u32[]{:S(2)}) %all-to-all-start.3) | async-done | bytes 65568 | tf_op jit(solution)/shard_map/all_to_all | solution.py:9
  232.5 5.7 %reduce-scatter.2.cloned.1.call-done = bf16[128,256]{1,0:T(8,128)(2,1)} async-done(((bf16[4096,256]{1,0:T(8,128)(2,1)}), bf16[128,256]{1,0:T(8,128)(2,1)}) %reduce-scatter.2.cloned.1.call-update) | async-done | bytes 65552 | tf_op jit(solution)/shard_map/reduce_scatter | solution.py:150
  238.1 1.6 broadcast_in_dim.82
  239.7 4.1 %all-to-all-start.4 = ((bf16[4,128,256]{2,1,0:T(8,128)(2,1)}), bf16[4,128,256]{2,1,0:T(8,128)(2,1)S(1)}, u32[]{:S(2)}, u32[]{:S(2)}) async-start(bf16[4,128,256]{2,1,0:T(8,128)(2,1)} %broadcast_in_dim.82), calls=%async_computation.5 | async-start | bytes 524288 | tf_op jit(solution)/shard_map/all_to_all | solution.py:9
  243.8 2.3 fusion
  246.7 2.7 all-to-all-done.4
  250.0 31.5 %all-reduce.7.cloned.1.call-done = f32[256,256]{1,0:T(8,128)} async-done(((f32[256,256]{1,0:T(8,128)}), f32[256,256]{1,0:T(8,128)}) %all-reduce.7.cloned.1.call-update) | async-done | bytes 262160 | tf_op jit(solution)/shard_map/psum | solution.py:155
  281.6 1.7 copy.93
  (74 shorter events, 12.5 us)
Async XLA Ops:
  7.2 45.2 %copy-start = (bf16[4096,256]{1,0:T(8,128)(2,1)S(1)}, bf16[4096,256]{1,0:T(8,128)(2,1)}, u32[]{:S(2)}) copy-start(bf16[4096,256]{1,0:T(8,128)(2,1)} %param.21) | copy-start | bytes 6291460
  17.0 14.5 %copy-start.10 = (s32[64]{0:T(128)S(1)}, s32[64]{0:T(128)}, u32[]{:S(2)}) copy-start(s32[64]{0:T(128)} %param.14) | copy-start | bytes 772
  17.0 14.5 %copy-start.13 = (bf16[256]{0:T(256)(128)(2,1)S(1)}, bf16[256]{0:T(256)(128)(2,1)}, u32[]{:S(2)}) copy-start(bf16[256]{0:T(256)(128)(2,1)} %param.23) | copy-start | bytes 1540
  22.8 20.2 %all-to-all-start = ((bf16[32,2,4096]{2,1,0:T(2,128)(2,1)}), bf16[32,2,4096]{2,1,0:T(2,128)(2,1)S(1)}, u32[]{:S(2)}, u32[]{:S(2)}) async-start(bf16[32,2,4096]{2,1,0:T(2,128)(2,1)} %reshape.152), calls=%async_computation | async-start | bytes 1048576 | tf_op jit(solution)/shard_map/all_to_all | solution.py:140
  31.4 197.8 %all-reduce.5.cloned.1.call-start = ((), (), s32[]{:S(2)}) async-start(), calls=%async_computation.7 | async-start | bytes 524288 | tf_op jit(solution)/shard_map/psum | solution.py:156
  49.7 0.8 copy-start.9
  49.7 1.0 copy-start.12
  49.7 1.3 copy-start.8
  51.4 1.0 copy-start.5
  51.7 1.2 copy-start.3
  52.4 0.8 copy-start.7
  52.4 1.0 copy-start.11
  55.6 182.5 %reduce-scatter.2.cloned.1.call-start = ((), (), s32[]{:S(2)}) async-start(), calls=%async_computation.6 | async-start | bytes 2162688 | tf_op jit(solution)/shard_map/reduce_scatter | solution.py:150
  61.4 10.5 %all-to-all-start.1 = ((f32[32,1,128]{2,1,0:T(1,128)}), f32[32,1,128]{2,1,0:T(1,128)S(1)}, u32[]{:S(2)}, u32[]{:S(2)}) async-start(f32[32,1,128]{2,1,0:T(1,128)} %broadcast_in_dim.45), calls=%async_computation.1 | async-start | bytes 32768 | tf_op jit(solution)/shard_map/all_to_all | solution.py:9
  65.1 2.9 copy-start.1
  65.1 3.1 %copy-start.6 = (f32[64,128,32]{1,2,0:T(8,128)S(1)}, f32[64,128,32]{1,2,0:T(8,128)}, u32[]{:S(2)}) copy-start(f32[64,128,32]{1,2,0:T(8,128)} %copy-done.5) | copy-start | bytes 3145732
  67.9 1.3 copy-start.4
  72.0 149.9 %all-to-all-start.2 = ((bf16[64,128,32]{1,2,0:T(8,128)(2,1)}), bf16[64,128,32]{1,2,0:T(8,128)(2,1)S(1)}, u32[]{:S(2)}, u32[]{:S(2)}) async-start(bf16[64,128,32]{1,2,0:T(8,128)(2,1)} %gather_fusion.3), calls=%async_computation.2 | async-start | bytes 1048576 | tf_op jit(solution)/shard_map/all_to_all | solution.py:145
  78.7 1.9 copy-start.2
  224.7 7.7 %all-to-all-start.3 = ((bf16[4,2,128,32]{2,3,1,0:T(8,128)(2,1)}), bf16[4,2,128,32]{2,3,1,0:T(8,128)(2,1)S(1)}, u32[]{:S(2)}, u32[]{:S(2)}) async-start(bf16[4,2,128,32]{2,3,1,0:T(8,128)(2,1)} %broadcast_in_dim.49), calls=%async_computation.3 | async-start | bytes 131072 | tf_op jit(solution)/shard_map/all_to_all | solution.py:9
  228.0 53.6 %all-reduce.7.cloned.1.call-start = ((), (), s32[]{:S(2)}) async-start(), calls=%async_computation.8 | async-start | bytes 524288 | tf_op jit(solution)/shard_map/psum | solution.py:155
  239.7 9.7 %all-to-all-start.4 = ((bf16[4,128,256]{2,1,0:T(8,128)(2,1)}), bf16[4,128,256]{2,1,0:T(8,128)(2,1)S(1)}, u32[]{:S(2)}, u32[]{:S(2)}) async-start(bf16[4,128,256]{2,1,0:T(8,128)(2,1)} %broadcast_in_dim.82), calls=%async_computation.5 | async-start | bytes 524288 | tf_op jit(solution)/shard_map/all_to_all | solution.py:9
Sparse Core Ops, SparseCore 0:
  55.8 101.8 all-reduce.4
  161.2 76.8 reduce-scatter.1
  240.5 41.0 all-reduce.6
